TPU v7x, 32 devices: a whole 2x2x4 slice. The times are simulated.
32 devices in a mesh: groups: 2 (over x), expert: 16 (over z, y, core).
Axes of the slice: x: 2, y: 2, z: 4, core: 2. Of those that a mesh axis runs over, the one named last changes fastest.
Arguments:
- hidden_in: bfloat16 [4096, 2048], P(('groups', 'expert')), parts along dimension 0, may hold values from -6 to 6
- norm_gain: float32 [2048], replicated, may hold values from 0.1 to 1.9
- router_weight: bfloat16 [2048, 16], replicated, may hold values from -0.125 to 0.125
- expert_ids: int32 [4096, 8], P(('groups', 'expert')), parts along dimension 0, may hold values from 0 to 15, all different within a row; in each aligned block of 128 rows (0 to 127, 128 to 255, ...) at most 96 rows name the same one
- w_gate: bfloat16 [16, 2048, 768], P('expert'), may hold values from -0.125 to 0.125
- w_up: bfloat16 [16, 2048, 768], P('expert'), may hold values from -0.125 to 0.125
- w_down: bfloat16 [16, 768, 2048], P('expert'), may hold values from -0.21875 to 0.21875
Outputs:
- combined: bfloat16 [4096, 2048], P(('groups', 'expert')), parts along dimension 0
There are 2 independent parts, one for each index of `groups`. A program takes and returns all parts, laid end to end along the dimension named above; an argument that names none is the same for every part. Nothing has to cross between parts.
Inputs may be any that keep to these rules, and one draw needn't show every extreme that they name: `expert_ids`: each row names 8 different experts; within each aligned block of 128 rows (the rows of one device) no expert is named by more than 96 rows, a bound that some block reaches.
All inputs are finite; a program needn't handle non-finite values.
Results may differ from a plain program's by a relative error of at most 0.0074.
Values may be sent and summed in bfloat16 or wider, within the bound.
A program may use at most 128 MiB of HBM per device.

v0:
```python
import jax
import jax.numpy as jnp
from jax import lax
from jax.sharding import PartitionSpec as P


def local(hidden_in, norm_gain, router_weight, expert_ids, w_gate, w_up, w_down):
    tok_rows = hidden_in.shape[0]
    top_count = expert_ids.shape[1]
    num_experts = router_weight.shape[1]
    dev_count = lax.axis_size("expert")
    local_experts = w_gate.shape[0]
    cap_rows = tok_rows * top_count * 3 // (2 * num_experts)
    as_float = hidden_in.astype(jnp.float32)
    inv_rms = lax.rsqrt(jnp.mean(as_float * as_float, axis=1, keepdims=True) + 1e-06)
    normed = (as_float * inv_rms * norm_gain).astype(jnp.bfloat16)
    logits = jnp.dot(normed, router_weight, preferred_element_type=jnp.float32)
    exp_logits = jnp.exp(logits)
    expert_iota = jnp.arange(num_experts, dtype=jnp.int32)
    choice_hot = (expert_ids[:, :, None] == expert_iota[None, None, :]).astype(jnp.float32)
    picked = jnp.sum(choice_hot * exp_logits[:, None, :], axis=2)
    route_w = picked / jnp.sum(picked, axis=1, keepdims=True)
    flat_ids = expert_ids.reshape(-1)
    onehot = (flat_ids[:, None] == expert_iota[None, :]).astype(jnp.int32)
    before = jnp.cumsum(onehot, axis=0) - onehot
    slot_index = jnp.sum(before * onehot, axis=1)
    dest_index = (
        flat_ids // local_experts * cap_rows + slot_index
    ) * local_experts + flat_ids % local_experts
    token_rows = jnp.repeat(normed, top_count, axis=0)
    outgoing = (
        jnp.zeros((num_experts * cap_rows, normed.shape[1]), jnp.bfloat16)
        .at[dest_index]
        .set(token_rows)
    )
    outgoing = outgoing.reshape(dev_count, cap_rows, local_experts, normed.shape[1])
    arrived = lax.all_to_all(outgoing, "expert", split_axis=0, concat_axis=0, tiled=True)
    gate_act = jnp.einsum("smed,edf->smef", arrived, w_gate, preferred_element_type=jnp.float32)
    up_act = jnp.einsum("smed,edf->smef", arrived, w_up, preferred_element_type=jnp.float32)
    hidden = (jax.nn.silu(gate_act) * up_act).astype(jnp.bfloat16)
    returned = lax.all_to_all(
        jnp.einsum("smef,efd->smed", hidden, w_down, preferred_element_type=jnp.float32).astype(
            jnp.bfloat16
        ),
        "expert",
        split_axis=0,
        concat_axis=0,
        tiled=True,
    )
    returned = returned.reshape(num_experts * cap_rows, normed.shape[1])
    gathered = returned[dest_index].reshape(tok_rows, top_count, normed.shape[1])
    combined = jnp.sum(gathered.astype(jnp.float32) * route_w[:, :, None], axis=1).astype(
        jnp.bfloat16
    )
    return combined


def solution(mesh):
    in_specs = (
        P(("groups", "expert"), None),
        P(),
        P(),
        P(("groups", "expert"), None),
        P("expert", None, None),
        P("expert", None, None),
        P("expert", None, None),
    )
    out_specs = P(("groups", "expert"), None)
    return jax.shard_map(local, mesh=mesh, in_specs=in_specs, out_specs=out_specs, check_vma=False)
```

profile of v0, /device:TPU:15, one launch (start us, length us, event | category | flops | bytes accessed | tf_op | source)
XLA Modules:
  0.0 354.0 jit_solution(13436347442580943173)
XLA Ops:
  0.0 0.0 copy-start
  0.0 0.8 broadcast_multiply_fusion
  0.8 0.9 copy.28
  1.7 0.1 eq.44
  1.8 0.1 eq.40
  1.9 1.2 fusion.29
  3.2 0.1 copy.27
  3.3 0.1 mul.63
  3.4 4.5 %reduce-window.6 = s32[16,8,128]{2,1,0:T(8,128)S(1)} reduce-window(s32[16,8,128]{2,1,0:T(8,128)S(1)} %fusion.35, s32[]{:T(128)} %constant.40.clone.1), window={size=1x1x128 pad=0_0x0_0x127_0}, to_apply=%region_0.0 | reduce-window | flops 2080768 | bytes 131076 | tf_op jit(solution)/shard_map/reduce-window
  7.9 0.1 slice.10
  8.0 0.1 copy.30
  8.2 0.1 copy.31
  8.2 0.1 broadcast_add_fusion
  8.4 2.0 fusion.31
  10.4 10.7 %scatter_custom_fusion = bf16[1536,2048]{1,0:T(8,128)(2,1)} fusion(s32[1024]{0:T(1024)S(1)} %bitcast.108, bf16[]{:T(256)} %constant.38.clone.1, bf16[128,2048]{1,0:T(8,128)(2,1)} %fusion.31), kind=kCustom, calls=%fused_computation.16 | custom fusion | bytes 6815746 | tf_op jit(solution)/shard_map/scatter | solution.py:34
  21.1 0.0 copy-start.4
  21.1 144.0 %all_to_all.10 = bf16[16,96,1,2048]{3,1,2,0:T(8,128)(2,1)S(1)} all-to-all(bf16[16,96,1,2048]{3,1,2,0:T(8,128)(2,1)} %bitcast.104), channel_id=1, replica_groups=mesh['groups'=2,'expert'=16] {'expert'}, dimensions={0} | all-to-all | bytes 12582912 | tf_op jit(solution)/shard_map/all_to_all | solution.py:37
  165.1 0.0 copy-start.1
  165.1 2.7 copy-done.1
  167.7 0.0 copy-done.4
  167.7 6.6 %fusion.1 = f32[16,96,768]{2,1,0:T(8,128)} fusion(bf16[16,96,1,2048]{3,1,2,0:T(8,128)(2,1)S(1)} %all_to_all.10, bf16[1,2048,768]{2,1,0:T(8,128)(2,1)S(1)} %copy-done.4), kind=kOutput, calls=%fused_computation.4 | convolution fusion | flops 4831838208 | bytes 14155776 | tf_op jit(solution)/shard_map/smed,edf->smef/dot_general | solution.py:39
  174.3 0.0 copy-done
  174.3 16.8 %convert_bitcast_fusion = bf16[16,96,1,2048]{3,1,2,0:T(8,128)(2,1)} fusion(bf16[1,768,2048]{2,1,0:T(8,128)(2,1)S(1)} %copy-done, f32[16,96,768]{2,1,0:T(8,128)} %fusion.1, bf16[1,2048,768]{2,1,0:T(8,128)(2,1)} %param.11, bf16[16,96,1,2048]{3,1,2,0:T(8,128)(2,1)} %copy-done.1), kind=kOutput, calls=%fused_computation.8 | convolution fusion | flops 9673900032 | bytes 23592960 | tf_op jit(solution)/shard_map/smef,efd->smed/dot_general | solution.py:42
  191.2 0.0 copy-start.2
  191.2 5.6 %all-to-all-start.1 = ((bf16[16,96,1,2048]{3,1,2,0:T(8,128)(2,1)}), bf16[16,96,1,2048]{3,1,2,0:T(8,128)(2,1)}, u32[]{:S(2)}, u32[]{:S(2)}) async-start(bf16[16,96,1,2048]{3,1,2,0:T(8,128)(2,1)} %convert_bitcast_fusion), calls=%async_computation.1 | async-start | bytes 12582912 | tf_op jit(solution)/shard_map/all_to_all | solution.py:41
  196.8 0.0 copy-done.2
  196.8 1.3 convolution_exponential_fusion
  198.1 0.0 copy-done.3
  198.2 0.1 copy.33
  198.3 135.9 %all-to-all-done.1 = bf16[16,96,1,2048]{3,1,2,0:T(8,128)(2,1)} async-done(((bf16[16,96,1,2048]{3,1,2,0:T(8,128)(2,1)}), bf16[16,96,1,2048]{3,1,2,0:T(8,128)(2,1)}, u32[]{:S(2)}, u32[]{:S(2)}) %all-to-all-start.1) | async-done | bytes 6291488 | tf_op jit(solution)/shard_map/all_to_all | solution.py:41
  334.2 12.4 %gather_fusion = bf16[1024,2048]{1,0:T(8,128)(2,1)} fusion(bf16[1536,2048]{1,0:T(8,128)(2,1)} %bitcast.26, s32[1024]{0:T(1024)S(1)} %broadcast_clamp_fusion), kind=kCustom, calls=%fused_computation | custom fusion | bytes 8392704 | tf_op jit(solution)/shard_map/gather | solution.py:51
  346.7 7.3 %fusion = bf16[128,2048]{1,0:T(8,128)(2,1)} fusion(bf16[1024,2048]{1,0:T(8,128)(2,1)} %gather_fusion, f32[128,8]{1,0:T(8,128)S(1)} %copy.33), kind=kLoop, calls=%fused_computation.3 | loop fusion | flops 6029312 | bytes 4722688 | tf_op jit(solution)/shard_map/reduce_sum | solution.py:52
  (10 shorter events, 0.1 us)
Async XLA Ops:
  0.0 174.3 %copy-start = (bf16[1,768,2048]{2,1,0:T(8,128)(2,1)S(1)}, bf16[1,768,2048]{2,1,0:T(8,128)(2,1)}, u32[]{:S(2)}) copy-start(bf16[1,768,2048]{2,1,0:T(8,128)(2,1)} %param.13) | copy-start | bytes 9437188
  21.1 146.7 %copy-start.4 = (bf16[1,2048,768]{2,1,0:T(8,128)(2,1)S(1)}, bf16[1,2048,768]{2,1,0:T(8,128)(2,1)}, u32[]{:S(2)}) copy-start(bf16[1,2048,768]{2,1,0:T(8,128)(2,1)} %param.12) | copy-start | bytes 9437188
  165.1 2.7 copy-start.1
  191.2 5.6 %copy-start.2 = (bf16[2048,16]{0,1:T(8,128)(2,1)S(1)}, bf16[2048,16]{0,1:T(8,128)(2,1)}, u32[]{:S(2)}) copy-start(bf16[2048,16]{0,1:T(8,128)(2,1)} %param.9) | copy-start | bytes 196612
  191.2 6.9 %copy-start.3 = (s32[128,8]{0,1:T(8,128)S(1)}, s32[128,8]{0,1:T(8,128)}, u32[]{:S(2)}) copy-start(s32[128,8]{0,1:T(8,128)} %param.10) | copy-start | bytes 12292
  191.2 143.1 %all-to-all-start.1 = ((bf16[16,96,1,2048]{3,1,2,0:T(8,128)(2,1)}), bf16[16,96,1,2048]{3,1,2,0:T(8,128)(2,1)}, u32[]{:S(2)}, u32[]{:S(2)}) async-start(bf16[16,96,1,2048]{3,1,2,0:T(8,128)(2,1)} %convert_bitcast_fusion), calls=%async_computation.1 | async-start | bytes 12582912 | tf_op jit(solution)/shard_map/all_to_all | solution.py:41
where the time goes:
time: 354 us
  blocking collectives  144 us (41%)
  waiting for transfers between devices  136 us (38%)
  local copies, waits for them, and re-layouts  27.4 us (8%)
  matrix products  24.7 us (7%)
  other arithmetic  16.2 us (5%)
  starting transfers between devices  5.64 us (2%)
    all_to_all x1, blocking collectives, local(): lax.all_to_all(outgoing, 'expert', split_axis=0, concat_axis=0, tiled=True)  144 us
    all_to_all x1, waiting for transfers between devices, local(): lax.all_to_all(jnp.einsum('smef,efd->smed', hidden, w_down, preferred_ele...  136 us
    dot_general x1, matrix products, local(): jnp.einsum('smef,efd->smed', hidden, w_down, preferred_element_type=jnp.f...  16.8 us
    gather x1, local copies, waits for them, and re-layouts, local(): returned[dest_index].reshape(tok_rows, top_count, normed.shape[1])  12.4 us
    scatter x1, local copies, waits for them, and re-layouts, local(): outgoing = jnp.zeros((num_experts * cap_rows, normed.shape[1]), jnp.bfloa...  10.7 us
    reduce_sum x1, other arithmetic, local(): jnp.sum(gathered.astype(jnp.float32) * route_w[:, :, None], axis=1)  7.32 us
  transfers between devices with their start and end apart: 1, of which 1 were waited for; matrix products, arithmetic and copies ran while one was open for 0% of the time, Pallas kernels for 0%

commit v1 on v0

--- a/solution.py
+++ b/solution.py
@@ -38,15 +38,18 @@
     gate_act = jnp.einsum("smed,edf->smef", arrived, w_gate, preferred_element_type=jnp.float32)
     up_act = jnp.einsum("smed,edf->smef", arrived, w_up, preferred_element_type=jnp.float32)
     hidden = (jax.nn.silu(gate_act) * up_act).astype(jnp.bfloat16)
-    returned = lax.all_to_all(
-        jnp.einsum("smef,efd->smed", hidden, w_down, preferred_element_type=jnp.float32).astype(
-            jnp.bfloat16
-        ),
-        "expert",
-        split_axis=0,
-        concat_axis=0,
-        tiled=True,
+    shard = jnp.einsum("smef,efd->smed", hidden, w_down, preferred_element_type=jnp.float32).astype(
+        jnp.bfloat16
     )
+    ways, here = (lax.axis_size("expert"), lax.axis_index("expert"))
+    width = shard.shape[0] // ways
+    turned = jnp.roll(shard, -here * width, axis=0)
+    got = [lax.slice_in_dim(turned, 0, width, axis=0)]
+    for far in range(1, ways):
+        sent = lax.slice_in_dim(turned, far * width, (far + 1) * width, axis=0)
+        got.append(lax.ppermute(sent, "expert", [(d, (d + far) % ways) for d in range(ways)]))
+    line = jnp.concatenate(got[::-1], axis=0)
+    returned = jnp.roll(line, (here + 1) * got[0].shape[0], axis=0)
     returned = returned.reshape(num_experts * cap_rows, normed.shape[1])
     gathered = returned[dest_index].reshape(tok_rows, top_count, normed.shape[1])
     combined = jnp.sum(gathered.astype(jnp.float32) * route_w[:, :, None], axis=1).astype(

time: 354 us -> 399 us (1.13)
  the two profiles are of different devices: /device:TPU:15 before, /device:TPU:0 now
where the time goes in v1:
time: 399 us
  waiting for transfers between devices  218 us (55%)
  starting transfers between devices  95.8 us (24%)
  local copies, waits for them, and re-layouts  32.2 us (8%)
  matrix products  27.6 us (7%)
  other arithmetic  25.1 us (6%)
    all_to_all x1, waiting for transfers between devices, local(): lax.all_to_all(outgoing, 'expert', split_axis=0, concat_axis=0, tiled=True)  113 us
    ppermute x15, waiting for transfers between devices, local(): lax.ppermute(sent, 'expert', [(d, (d + far) % ways) for d in range(ways)])  105 us
    ppermute x15, starting transfers between devices, local(): lax.ppermute(sent, 'expert', [(d, (d + far) % ways) for d in range(ways)])  88.2 us
    dot_general x1, matrix products, local(): jnp.einsum('smef,efd->smed', hidden, w_down, preferred_element_type=jnp.f...  16.9 us
    gather x1, local copies, waits for them, and re-layouts, local(): returned[dest_index].reshape(tok_rows, top_count, normed.shape[1])  12.5 us
    scatter x1, local copies, waits for them, and re-layouts, local(): outgoing = jnp.zeros((num_experts * cap_rows, normed.shape[1]), jnp.bfloa...  10.7 us
    dot_general x1, matrix products, local(): jnp.einsum('smed,edf->smef', arrived, w_up, preferred_element_type=jnp.fl...  9.46 us
  transfers between devices with their start and end apart: 16, of which 10 were waited for; matrix products, arithmetic and copies ran while one was open for 1% of the time, Pallas kernels for 0%

profile of v1, /device:TPU:0, one launch (start us, length us, event | category | flops | bytes accessed | tf_op | source)
XLA Modules:
  0.0 398.7 jit_solution(12002354114780307763)
XLA Ops:
  0.8 0.9 copy.27
  1.9 1.2 fusion.31
  3.4 4.5 %reduce-window.6 = s32[16,8,128]{2,1,0:T(8,128)S(1)} reduce-window(s32[16,8,128]{2,1,0:T(8,128)S(1)} %fusion.37, s32[]{:T(128)} %constant.60.clone.1), window={size=1x1x128 pad=0_0x0_0x127_0}, to_apply=%region_0.0 | reduce-window | flops 2080768 | bytes 131076 | tf_op jit(solution)/shard_map/reduce-window
  8.4 2.0 fusion.33
  10.4 10.7 %scatter_custom_fusion = bf16[1536,2048]{1,0:T(8,128)(2,1)} fusion(s32[1024]{0:T(1024)S(1)} %bitcast.107, bf16[]{:T(256)} %constant.58.clone.1, bf16[128,2048]{1,0:T(8,128)(2,1)} %fusion.33), kind=kCustom, calls=%fused_computation.22 | custom fusion | bytes 6815746 | tf_op jit(solution)/shard_map/scatter | solution.py:34
  21.1 7.6 %all-to-all-start = ((bf16[16,96,1,2048]{3,1,2,0:T(8,128)(2,1)}), bf16[16,96,1,2048]{3,1,2,0:T(8,128)(2,1)}, u32[]{:S(2)}, u32[]{:S(2)}) async-start(bf16[16,96,1,2048]{3,1,2,0:T(8,128)(2,1)} %bitcast.103), calls=%async_computation | async-start | bytes 12582912 | tf_op jit(solution)/shard_map/all_to_all | solution.py:37
  28.7 1.3 convolution_exponential_fusion
  30.0 112.8 %all-to-all-done = bf16[16,96,1,2048]{3,1,2,0:T(8,128)(2,1)} async-done(((bf16[16,96,1,2048]{3,1,2,0:T(8,128)(2,1)}), bf16[16,96,1,2048]{3,1,2,0:T(8,128)(2,1)}, u32[]{:S(2)}, u32[]{:S(2)}) %all-to-all-start) | async-done | bytes 6291488 | tf_op jit(solution)/shard_map/all_to_all | solution.py:37
  142.8 9.5 %fusion.3 = f32[16,96,768]{2,1,0:T(8,128)} fusion(bf16[16,96,1,2048]{3,1,2,0:T(8,128)(2,1)} %all-to-all-done, bf16[1,2048,768]{2,1,0:T(8,128)(2,1)} %param.14), kind=kOutput, calls=%fused_computation.10 | convolution fusion | flops 4831838208 | bytes 14155776 | tf_op jit(solution)/shard_map/smed,edf->smef/dot_general | solution.py:39
  152.3 16.9 %convert_bitcast_fusion = bf16[16,96,1,2048]{3,1,0,2:T(8,128)(2,1)} fusion(bf16[1,768,2048]{2,1,0:T(8,128)(2,1)S(1)} %copy-done, f32[16,96,768]{2,1,0:T(8,128)} %fusion.3, bf16[1,2048,768]{2,1,0:T(8,128)(2,1)} %param.13, bf16[16,96,1,2048]{3,1,2,0:T(8,128)(2,1)} %all-to-all-done), kind=kOutput, calls=%fused_computation.14 | convolution fusion | flops 9673900032 | bytes 23592960 | tf_op jit(solution)/shard_map/smef,efd->smed/dot_general | solution.py:41
  169.2 4.7 %fusion.2 = bf16[16,96,1,2048]{3,1,0,2:T(8,128)(2,1)S(1)} fusion(s32[]{:T(128)S(6)} %select_n.37, bf16[16,96,1,2048]{3,1,0,2:T(8,128)(2,1)} %convert_bitcast_fusion), kind=kLoop, calls=%fused_computation.9 | loop fusion | flops 3145728 | bytes 12582916 | tf_op jit(solution)/shard_map/jit(_roll_dynamic)/concatenate | solution.py:46
  173.9 2.6 copy-done.2
  176.6 1.6 fusion.39
  178.2 26.6 %collective-permute-start = (bf16[1,96,1,2048]{3,1,0,2:T(8,128)(2,1)}, bf16[1,96,1,2048]{3,1,0,2:T(8,128)(2,1)}, u32[]{:S(2)}, u32[]{:S(2)}) collective-permute-start(bf16[1,96,1,2048]{3,1,0,2:T(8,128)(2,1)} %get-tuple-element.22), channel_id=1, source_target_pairs={{0,15},{1,0},{2,1},{3,2},{4,3},{5,4},{6,5},{7,6},{8,7},{9,8},{10,9... | collective-permute-start | bytes 1179656 | tf_op jit(solution)/shard_map/ppermute | solution.py:50
  205.9 1.8 collective-permute-start.13
  207.6 6.7 %collective-permute-done = bf16[1,96,1,2048]{3,1,0,2:T(8,128)(2,1)} collective-permute-done((bf16[1,96,1,2048]{3,1,0,2:T(8,128)(2,1)}, bf16[1,96,1,2048]{3,1,0,2:T(8,128)(2,1)}, u32[]{:S(2)}, u32[]{:S(2)}) %collective-permute-start) | collective-permute-done | bytes 393248 | tf_op jit(solution)/shard_map/ppermute | solution.py:50
  214.4 17.1 %collective-permute-start.2 = (bf16[1,96,1,2048]{3,1,0,2:T(8,128)(2,1)}, bf16[1,96,1,2048]{3,1,0,2:T(8,128)(2,1)S(1)}, u32[]{:S(2)}, u32[]{:S(2)}) collective-permute-start(bf16[1,96,1,2048]{3,1,0,2:T(8,128)(2,1)} %get-tuple-element.20), channel_id=1, source_target_pairs={{0,13},{1,14},{2,15},{3,0},{4,1},{5,2},{6,3},{7,4},{8,5},{9,6},{10... | collective-permute-start | bytes 1179656 | tf_op jit(solution)/shard_map/ppermute | solution.py:50
  231.5 1.0 constant_dynamic-update-slice_fusion.14
  232.5 7.9 %collective-permute-start.3 = (bf16[1,96,1,2048]{3,1,0,2:T(8,128)(2,1)}, bf16[1,96,1,2048]{3,1,0,2:T(8,128)(2,1)S(1)}, u32[]{:S(2)}, u32[]{:S(2)}) collective-permute-start(bf16[1,96,1,2048]{3,1,0,2:T(8,128)(2,1)} %get-tuple-element.19), channel_id=1, source_target_pairs={{0,12},{1,13},{2,14},{3,15},{4,0},{5,1},{6,2},{7,3},{8,4},{9,5},{1... | collective-permute-start | bytes 1179656 | tf_op jit(solution)/shard_map/ppermute | solution.py:50
  241.3 9.0 %collective-permute-done.3 = bf16[1,96,1,2048]{3,1,0,2:T(8,128)(2,1)S(1)} collective-permute-done((bf16[1,96,1,2048]{3,1,0,2:T(8,128)(2,1)}, bf16[1,96,1,2048]{3,1,0,2:T(8,128)(2,1)S(1)}, u32[]{:S(2)}, u32[]{:S(2)}) %collective-permute-start.3) | collective-permute-done | bytes 393248 | tf_op jit(solution)/shard_map/ppermute | solution.py:50
  250.3 8.4 %collective-permute-done.4 = bf16[1,96,1,2048]{3,1,0,2:T(8,128)(2,1)S(1)} collective-permute-done((bf16[1,96,1,2048]{3,1,0,2:T(8,128)(2,1)}, bf16[1,96,1,2048]{3,1,0,2:T(8,128)(2,1)S(1)}, u32[]{:S(2)}, u32[]{:S(2)}) %collective-permute-start.4) | collective-permute-done | bytes 393248 | tf_op jit(solution)/shard_map/ppermute | solution.py:50
  258.7 18.6 %collective-permute-start.6 = (bf16[1,96,1,2048]{3,1,0,2:T(8,128)(2,1)S(1)}, bf16[1,96,1,2048]{3,1,0,2:T(8,128)(2,1)S(1)}, u32[]{:S(2)}, u32[]{:S(2)}) collective-permute-start(bf16[1,96,1,2048]{3,1,0,2:T(8,128)(2,1)S(1)} %get-tuple-element.16), channel_id=1, source_target_pairs={{0,9},{1,10},{2,11},{3,12},{4,13},{5,14},{6,15},{7,0},{8,1},{9,2},... | collective-permute-start | bytes 1179656 | tf_op jit(solution)/shard_map/ppermute | solution.py:50
  277.4 15.9 %collective-permute-start.7 = (bf16[1,96,1,2048]{3,1,0,2:T(8,128)(2,1)S(1)}, bf16[1,96,1,2048]{3,1,0,2:T(8,128)(2,1)S(1)}, u32[]{:S(2)}, u32[]{:S(2)}) collective-permute-start(bf16[1,96,1,2048]{3,1,0,2:T(8,128)(2,1)S(1)} %get-tuple-element.15), channel_id=1, source_target_pairs={{0,8},{1,9},{2,10},{3,11},{4,12},{5,13},{6,14},{7,15},{8,0},{9,1},... | collective-permute-start | bytes 1179656 | tf_op jit(solution)/shard_map/ppermute | solution.py:50
  293.4 38.1 %collective-permute-done.7 = bf16[1,96,1,2048]{3,1,0,2:T(8,128)(2,1)S(1)} collective-permute-done((bf16[1,96,1,2048]{3,1,0,2:T(8,128)(2,1)S(1)}, bf16[1,96,1,2048]{3,1,0,2:T(8,128)(2,1)S(1)}, u32[]{:S(2)}, u32[]{:S(2)}) %collective-permute-start.7) | collective-permute-done | bytes 393248 | tf_op jit(solution)/shard_map/ppermute | solution.py:50
  331.6 2.7 collective-permute-done.8
  334.3 26.4 %collective-permute-done.9 = bf16[1,96,1,2048]{3,1,0,2:T(8,128)(2,1)S(1)} collective-permute-done((bf16[1,96,1,2048]{3,1,0,2:T(8,128)(2,1)S(1)}, bf16[1,96,1,2048]{3,1,0,2:T(8,128)(2,1)S(1)}, u32[]{:S(2)}, u32[]{:S(2)}) %collective-permute-start.9) | collective-permute-done | bytes 393248 | tf_op jit(solution)/shard_map/ppermute | solution.py:50
  360.7 4.1 %collective-permute-done.10 = bf16[1,96,1,2048]{3,1,0,2:T(8,128)(2,1)S(1)} collective-permute-done((bf16[1,96,1,2048]{3,1,0,2:T(8,128)(2,1)S(1)}, bf16[1,96,1,2048]{3,1,0,2:T(8,128)(2,1)S(1)}, u32[]{:S(2)}, u32[]{:S(2)}) %collective-permute-start.10) | collective-permute-done | bytes 393248 | tf_op jit(solution)/shard_map/ppermute | solution.py:50
  364.8 8.6 %collective-permute-done.11 = bf16[1,96,1,2048]{3,1,0,2:T(8,128)(2,1)S(1)} collective-permute-done((bf16[1,96,1,2048]{3,1,0,2:T(8,128)(2,1)S(1)}, bf16[1,96,1,2048]{3,1,0,2:T(8,128)(2,1)S(1)}, u32[]{:S(2)}, u32[]{:S(2)}) %collective-permute-start.11) | collective-permute-done | bytes 393248 | tf_op jit(solution)/shard_map/ppermute | solution.py:50
  373.6 1.0 slice_dynamic-update-slice_fusion
  374.6 4.2 %fusion.1 = bf16[16,96,1,2048]{3,1,0,2:T(8,128)(2,1)} fusion(s32[]{:T(128)S(6)} %select_n.39, bf16[16,96,1,2048]{3,1,0,2:T(8,128)(2,1)S(1)} %slice_dynamic-update-slice_fusion), kind=kLoop, calls=%fused_computation.8 | loop fusion | flops 3145728 | bytes 12582916 | tf_op jit(solution)/shard_map/jit(_roll_dynamic)/concatenate | solution.py:52
  378.8 12.5 %gather_fusion = bf16[1024,2048]{1,0:T(8,128)(2,1)} fusion(bf16[1536,2048]{1,0:T(8,128)(2,1)} %bitcast.102, s32[1024]{0:T(1024)S(1)} %broadcast_clamp_fusion), kind=kCustom, calls=%fused_computation | custom fusion | bytes 8392704 | tf_op jit(solution)/shard_map/gather | solution.py:54
  391.4 7.3 %fusion = bf16[128,2048]{1,0:T(8,128)(2,1)} fusion(bf16[1024,2048]{1,0:T(8,128)(2,1)} %gather_fusion, f32[128,8]{1,0:T(8,128)S(1)} %copy-done.3), kind=kLoop, calls=%fused_computation.7 | loop fusion | flops 6029312 | bytes 4722688 | tf_op jit(solution)/shard_map/reduce_sum | solution.py:55
  (60 shorter events, 4.1 us)
Async XLA Ops:
  0.0 152.3 %copy-start = (bf16[1,768,2048]{2,1,0:T(8,128)(2,1)S(1)}, bf16[1,768,2048]{2,1,0:T(8,128)(2,1)}, u32[]{:S(2)}) copy-start(bf16[1,768,2048]{2,1,0:T(8,128)(2,1)} %param.15) | copy-start | bytes 9437188
  21.1 7.6 %copy-start.4 = (bf16[2048,16]{0,1:T(8,128)(2,1)S(1)}, bf16[2048,16]{0,1:T(8,128)(2,1)}, u32[]{:S(2)}) copy-start(bf16[2048,16]{0,1:T(8,128)(2,1)} %param.11) | copy-start | bytes 196612
  21.1 8.9 %copy-start.5 = (s32[128,8]{0,1:T(8,128)S(1)}, s32[128,8]{0,1:T(8,128)}, u32[]{:S(2)}) copy-start(s32[128,8]{0,1:T(8,128)} %param.12) | copy-start | bytes 12292
  21.1 121.8 %all-to-all-start = ((bf16[16,96,1,2048]{3,1,2,0:T(8,128)(2,1)}), bf16[16,96,1,2048]{3,1,2,0:T(8,128)(2,1)}, u32[]{:S(2)}, u32[]{:S(2)}) async-start(bf16[16,96,1,2048]{3,1,2,0:T(8,128)(2,1)} %bitcast.103), calls=%async_computation | async-start | bytes 12582912 | tf_op jit(solution)/shard_map/all_to_all | solution.py:37
  173.9 2.6 copy-start.2
  178.2 36.2 %collective-permute-start = (bf16[1,96,1,2048]{3,1,0,2:T(8,128)(2,1)}, bf16[1,96,1,2048]{3,1,0,2:T(8,128)(2,1)}, u32[]{:S(2)}, u32[]{:S(2)}) collective-permute-start(bf16[1,96,1,2048]{3,1,0,2:T(8,128)(2,1)} %get-tuple-element.22), channel_id=1, source_target_pairs={{0,15},{1,0},{2,1},{3,2},{4,3},{5,4},{6,5},{7,6},{8,7},{9,8},{10,9... | collective-permute-start | bytes 1179656 | tf_op jit(solution)/shard_map/ppermute | solution.py:50
  205.6 26.9 %collective-permute-start.1 = (bf16[1,96,1,2048]{3,1,0,2:T(8,128)(2,1)}, bf16[1,96,1,2048]{3,1,0,2:T(8,128)(2,1)S(1)}, u32[]{:S(2)}, u32[]{:S(2)}) collective-permute-start(bf16[1,96,1,2048]{3,1,0,2:T(8,128)(2,1)} %get-tuple-element.21), channel_id=1, source_target_pairs={{0,14},{1,15},{2,0},{3,1},{4,2},{5,3},{6,4},{7,5},{8,6},{9,7},{10,... | collective-permute-start | bytes 1179656 | tf_op jit(solution)/shard_map/ppermute | solution.py:50
  205.6 167.9 %collective-permute-start.14 = (bf16[1,96,1,2048]{3,1,0,2:T(8,128)(2,1)S(1)}, bf16[1,96,1,2048]{3,1,0,2:T(8,128)(2,1)S(1)}, u32[]{:S(2)}, u32[]{:S(2)}) collective-permute-start(bf16[1,96,1,2048]{3,1,0,2:T(8,128)(2,1)S(1)} %get-tuple-element.8), channel_id=1, source_target_pairs={{0,1},{1,2},{2,3},{3,4},{4,5},{5,6},{6,7},{7,8},{8,9},{9,10},{10,1... | collective-permute-start | bytes 1179656 | tf_op jit(solution)/shard_map/ppermute | solution.py:50
  205.9 167.6 %collective-permute-start.13 = (bf16[1,96,1,2048]{3,1,0,2:T(8,128)(2,1)S(1)}, bf16[1,96,1,2048]{3,1,0,2:T(8,128)(2,1)S(1)}, u32[]{:S(2)}, u32[]{:S(2)}) collective-permute-start(bf16[1,96,1,2048]{3,1,0,2:T(8,128)(2,1)S(1)} %get-tuple-element.9), channel_id=1, source_target_pairs={{0,2},{1,3},{2,4},{3,5},{4,6},{5,7},{6,8},{7,9},{8,10},{9,11},{10,... | collective-permute-start | bytes 1179656 | tf_op jit(solution)/shard_map/ppermute | solution.py:50
  207.6 165.8 %collective-permute-start.12 = (bf16[1,96,1,2048]{3,1,0,2:T(8,128)(2,1)S(1)}, bf16[1,96,1,2048]{3,1,0,2:T(8,128)(2,1)S(1)}, u32[]{:S(2)}, u32[]{:S(2)}) collective-permute-start(bf16[1,96,1,2048]{3,1,0,2:T(8,128)(2,1)S(1)} %get-tuple-element.10), channel_id=1, source_target_pairs={{0,3},{1,4},{2,5},{3,6},{4,7},{5,8},{6,9},{7,10},{8,11},{9,12},{10... | collective-permute-start | bytes 1179656 | tf_op jit(solution)/shard_map/ppermute | solution.py:50
  214.4 26.9 %collective-permute-start.2 = (bf16[1,96,1,2048]{3,1,0,2:T(8,128)(2,1)}, bf16[1,96,1,2048]{3,1,0,2:T(8,128)(2,1)S(1)}, u32[]{:S(2)}, u32[]{:S(2)}) collective-permute-start(bf16[1,96,1,2048]{3,1,0,2:T(8,128)(2,1)} %get-tuple-element.20), channel_id=1, source_target_pairs={{0,13},{1,14},{2,15},{3,0},{4,1},{5,2},{6,3},{7,4},{8,5},{9,6},{10... | collective-permute-start | bytes 1179656 | tf_op jit(solution)/shard_map/ppermute | solution.py:50
  232.5 17.8 %collective-permute-start.3 = (bf16[1,96,1,2048]{3,1,0,2:T(8,128)(2,1)}, bf16[1,96,1,2048]{3,1,0,2:T(8,128)(2,1)S(1)}, u32[]{:S(2)}, u32[]{:S(2)}) collective-permute-start(bf16[1,96,1,2048]{3,1,0,2:T(8,128)(2,1)} %get-tuple-element.19), channel_id=1, source_target_pairs={{0,12},{1,13},{2,14},{3,15},{4,0},{5,1},{6,2},{7,3},{8,4},{9,5},{1... | collective-permute-start | bytes 1179656 | tf_op jit(solution)/shard_map/ppermute | solution.py:50
  241.3 17.4 %collective-permute-start.4 = (bf16[1,96,1,2048]{3,1,0,2:T(8,128)(2,1)}, bf16[1,96,1,2048]{3,1,0,2:T(8,128)(2,1)S(1)}, u32[]{:S(2)}, u32[]{:S(2)}) collective-permute-start(bf16[1,96,1,2048]{3,1,0,2:T(8,128)(2,1)} %get-tuple-element.18), channel_id=1, source_target_pairs={{0,11},{1,12},{2,13},{3,14},{4,15},{5,0},{6,1},{7,2},{8,3},{9,4},{... | collective-permute-start | bytes 1179656 | tf_op jit(solution)/shard_map/ppermute | solution.py:50
  250.3 27.0 %collective-permute-start.5 = (bf16[1,96,1,2048]{3,1,0,2:T(8,128)(2,1)}, bf16[1,96,1,2048]{3,1,0,2:T(8,128)(2,1)S(1)}, u32[]{:S(2)}, u32[]{:S(2)}) collective-permute-start(bf16[1,96,1,2048]{3,1,0,2:T(8,128)(2,1)} %get-tuple-element.17), channel_id=1, source_target_pairs={{0,10},{1,11},{2,12},{3,13},{4,14},{5,15},{6,0},{7,1},{8,2},{9,3},... | collective-permute-start | bytes 1179656 | tf_op jit(solution)/shard_map/ppermute | solution.py:50
  258.7 34.6 %collective-permute-start.6 = (bf16[1,96,1,2048]{3,1,0,2:T(8,128)(2,1)S(1)}, bf16[1,96,1,2048]{3,1,0,2:T(8,128)(2,1)S(1)}, u32[]{:S(2)}, u32[]{:S(2)}) collective-permute-start(bf16[1,96,1,2048]{3,1,0,2:T(8,128)(2,1)S(1)} %get-tuple-element.16), channel_id=1, source_target_pairs={{0,9},{1,10},{2,11},{3,12},{4,13},{5,14},{6,15},{7,0},{8,1},{9,2},... | collective-permute-start | bytes 1179656 | tf_op jit(solution)/shard_map/ppermute | solution.py:50
  277.4 54.2 %collective-permute-start.7 = (bf16[1,96,1,2048]{3,1,0,2:T(8,128)(2,1)S(1)}, bf16[1,96,1,2048]{3,1,0,2:T(8,128)(2,1)S(1)}, u32[]{:S(2)}, u32[]{:S(2)}) collective-permute-start(bf16[1,96,1,2048]{3,1,0,2:T(8,128)(2,1)S(1)} %get-tuple-element.15), channel_id=1, source_target_pairs={{0,8},{1,9},{2,10},{3,11},{4,12},{5,13},{6,14},{7,15},{8,0},{9,1},... | collective-permute-start | bytes 1179656 | tf_op jit(solution)/shard_map/ppermute | solution.py:50
  293.3 40.9 %collective-permute-start.8 = (bf16[1,96,1,2048]{3,1,0,2:T(8,128)(2,1)S(1)}, bf16[1,96,1,2048]{3,1,0,2:T(8,128)(2,1)S(1)}, u32[]{:S(2)}, u32[]{:S(2)}) collective-permute-start(bf16[1,96,1,2048]{3,1,0,2:T(8,128)(2,1)S(1)} %get-tuple-element.14), channel_id=1, source_target_pairs={{0,7},{1,8},{2,9},{3,10},{4,11},{5,12},{6,13},{7,14},{8,15},{9,0},... | collective-permute-start | bytes 1179656 | tf_op jit(solution)/shard_map/ppermute | solution.py:50
  331.5 29.1 %collective-permute-start.9 = (bf16[1,96,1,2048]{3,1,0,2:T(8,128)(2,1)S(1)}, bf16[1,96,1,2048]{3,1,0,2:T(8,128)(2,1)S(1)}, u32[]{:S(2)}, u32[]{:S(2)}) collective-permute-start(bf16[1,96,1,2048]{3,1,0,2:T(8,128)(2,1)S(1)} %get-tuple-element.13), channel_id=1, source_target_pairs={{0,6},{1,7},{2,8},{3,9},{4,10},{5,11},{6,12},{7,13},{8,14},{9,15},... | collective-permute-start | bytes 1179656 | tf_op jit(solution)/shard_map/ppermute | solution.py:50
  334.2 30.6 %collective-permute-start.10 = (bf16[1,96,1,2048]{3,1,0,2:T(8,128)(2,1)S(1)}, bf16[1,96,1,2048]{3,1,0,2:T(8,128)(2,1)S(1)}, u32[]{:S(2)}, u32[]{:S(2)}) collective-permute-start(bf16[1,96,1,2048]{3,1,0,2:T(8,128)(2,1)S(1)} %get-tuple-element.12), channel_id=1, source_target_pairs={{0,5},{1,6},{2,7},{3,8},{4,9},{5,10},{6,11},{7,12},{8,13},{9,14},{... | collective-permute-start | bytes 1179656 | tf_op jit(solution)/shard_map/ppermute | solution.py:50
  360.7 12.7 %collective-permute-start.11 = (bf16[1,96,1,2048]{3,1,0,2:T(8,128)(2,1)S(1)}, bf16[1,96,1,2048]{3,1,0,2:T(8,128)(2,1)S(1)}, u32[]{:S(2)}, u32[]{:S(2)}) collective-permute-start(bf16[1,96,1,2048]{3,1,0,2:T(8,128)(2,1)S(1)} %get-tuple-element.11), channel_id=1, source_target_pairs={{0,4},{1,5},{2,6},{3,7},{4,8},{5,9},{6,10},{7,11},{8,12},{9,13},{1... | collective-permute-start | bytes 1179656 | tf_op jit(solution)/shard_map/ppermute | solution.py:50
  378.8 12.5 %copy-start.3 = (f32[128,8]{1,0:T(8,128)S(1)}, f32[128,8]{1,0:T(8,128)}, u32[]{:S(2)}) copy-start(f32[128,8]{1,0:T(8,128)} %copy.31) | copy-start | bytes 12292
  378.8 19.9 %copy-start.1 = (bf16[1,768,2048]{2,1,0:T(8,128)(2,1)S(1)}, bf16[1,768,2048]{2,1,0:T(8,128)(2,1)}, u32[]{:S(2)}) copy-start(bf16[1,768,2048]{2,1,0:T(8,128)(2,1)} %param.15) | copy-start | bytes 9437188
